TPU v7x, 256 devices: a whole 4x4x8 slice. The times are simulated.
256 devices in a mesh: blk: 32 (over z_hi, x, core), grp: 8 (over z_lo, y).
Axes of the slice: x: 4, y: 4, z: 8 (z_hi: 4, z_lo: 2; z = z_hi * 2 + z_lo), core: 2. Of those that a mesh axis runs over, the one named last changes fastest.
Arguments:
- inv_tiles: bfloat16 [64, 64, 512, 512], P(None, 'grp', 'blk'), may hold values from -6 to 6
- factor: bfloat16 [8, 16, 512, 512], P('grp', None, 'blk'), may hold values from -0.0625 to 0.0625
- diag_inv_factor: float32 [8, 512, 512], P('grp', 'blk'), may hold values from -6 to 6
- structure: int32 [8, 16], replicated, may hold values from 0 to 63, as said below
Outputs:
- offdiag_inv: bfloat16 [8, 16, 512, 512], P('grp', None, 'blk')
- diag_inv: float32 [8, 512, 512], P('grp', 'blk')
Inputs may be any that keep to these rules, and one draw needn't show every extreme that they name: `structure`: each row lists 16 distinct ancestor blocks in ascending order, exactly 2 in each run of 8 blocks that starts at a multiple of 8; block 63 is listed in every row.
All inputs are finite; a program needn't handle non-finite values.
Results may differ from a plain program's by a relative error of at most 0.018.
Values may be sent and summed in bfloat16 or wider, within the bound.
A program may use at most 128 MiB of HBM per device.

v0:
```python
import jax
import jax.numpy as jnp
from jax import lax
from jax.sharding import PartitionSpec as P


def split_up(shard, dim, count):
    dims = shard.shape
    tiles = shard.reshape(*dims[:dim], count, dims[dim] // count, *dims[dim + 1 :])
    return jnp.moveaxis(tiles, dim, 0)


def sum_at_owner(shard, axis, dim):
    count = lax.axis_size(axis)
    tiles = lax.all_to_all(split_up(shard, dim, count), axis, 0, 0, tiled=True)
    return jnp.sum(tiles.astype(jnp.float32), axis=0)


def on_device(inv_tiles, factor, diag_inv_factor, structure):
    grp_count = lax.axis_size("grp")
    grp_index = lax.axis_index("grp")
    col_local = inv_tiles.shape[1]
    width = inv_tiles.shape[3]
    own_count = factor.shape[0]
    listed_count = factor.shape[1]
    slab_rows = factor.shape[2]
    per_group = listed_count // grp_count
    node_total = own_count * grp_count
    grouped = factor.reshape(own_count, grp_count, per_group, slab_rows, width)
    received = lax.all_to_all(grouped, "grp", split_axis=1, concat_axis=0, tiled=True)
    received = received.reshape(node_total, per_group, slab_rows, width)
    readers = lax.all_gather(received, "blk", axis=2, tiled=True)
    col_base = grp_index * col_local
    local_cols = lax.dynamic_slice_in_dim(structure, grp_index * per_group, per_group, 1) - col_base
    selected = inv_tiles[structure[:, :, None], local_cols[:, None, :]]
    summed = sum_at_owner(
        jnp.einsum(
            "crjxy,cjyz->crxz", selected, readers, preferred_element_type=jnp.float32
        ).astype(jnp.bfloat16),
        "grp",
        0,
    )
    offdiag = (-summed).astype(jnp.bfloat16)
    correction = sum_at_owner(
        jnp.einsum("krxy,krxz->ykz", factor, offdiag, preferred_element_type=jnp.float32).astype(
            jnp.bfloat16
        ),
        "blk",
        0,
    )
    diag_inv = diag_inv_factor - jnp.transpose(correction, (1, 0, 2))
    return (offdiag, diag_inv)


def solution(mesh):
    return jax.shard_map(
        on_device,
        mesh=mesh,
        in_specs=(
            P(None, "grp", "blk", None),
            P("grp", None, "blk", None),
            P("grp", "blk", None),
            P(),
        ),
        out_specs=(P("grp", None, "blk", None), P("grp", "blk", None)),
        check_vma=False,
    )
```

profile of v0, /device:TPU:1, one launch (start us, length us, event | category | flops | bytes accessed | tf_op | source)
XLA Modules:
  0.0 173.3 jit_solution(4277369298304297157)
XLA Ops:
  7.2 0.0 all-gather.3.cloned.1.call-start
  7.2 12.6 %all_to_all.19 = bf16[1,8,2,16,512]{4,3,2,0,1:T(8,128)(2,1)} all-to-all(bf16[1,8,2,16,512]{4,3,2,0,1:T(8,128)(2,1)} %bitcast.46), channel_id=1, replica_groups=mesh['blk'=32,'grp'=8] {'grp'}, dimensions={1} | all-to-all | bytes 524288 | tf_op jit(solution)/shard_map/all_to_all | solution.py:30
  19.8 0.0 all-gather.3.cloned.1.call-update
  19.8 0.8 fusion.13
  20.6 0.7 fusion.11
  21.3 0.1 broadcast_or_fusion
  21.4 0.1 reshape.63
  21.5 6.5 %gather_fusion = bf16[256,16,512]{2,1,0:T(8,128)(2,1)} fusion(bf16[64,8,16,512]{3,2,1,0:T(8,128)(2,1)} %param.4, s32[256]{0:T(256)S(1)} %reshape.63), kind=kCustom, calls=%fused_computation | custom fusion | bytes 8390656 | tf_op jit(solution)/shard_map/gather | solution.py:35
  28.0 69.7 %all-gather.3.cloned.1.call-done = bf16[1,8,2,512,512]{4,3,2,1,0:T(8,128)(2,1)} async-done(((bf16[1,8,2,16,512]{4,3,2,1,0:T(8,128)(2,1)}), bf16[1,8,2,512,512]{4,3,2,1,0:T(8,128)(2,1)}) %all-gather.3.cloned.1.call-update) | async-done | bytes 8388624 | tf_op jit(solution)/shard_map/all_gather | solution.py:32
  97.7 7.0 %fusion.4 = bf16[8,1,16,16,512]{4,3,2,1,0:T(8,128)(2,1)S(1)} fusion(bf16[8,16,2,16,512]{4,3,2,1,0:T(8,128)(2,1)} %bitcast.45, bf16[1,8,2,512,512]{4,3,2,1,0:T(8,128)(2,1)} %all-gather.3.cloned.1.call-done), kind=kOutput, calls=%fused_computation.5 | convolution fusion | flops 2148532224 | bytes 14680064 | tf_op jit(solution)/shard_map/crjxy,cjyz->crxz/dot_general | solution.py:37
  104.7 0.0 copy-start
  104.7 33.1 %all_to_all.20 = bf16[8,1,16,16,512]{4,3,2,1,0:T(8,128)(2,1)S(1)} all-to-all(bf16[8,1,16,16,512]{4,3,2,1,0:T(8,128)(2,1)S(1)} %fusion.4), channel_id=1, replica_groups=mesh['blk'=32,'grp'=8] {'grp'}, dimensions={0} | all-to-all | bytes 4194304 | tf_op jit(solution)/shard_map/all_to_all | solution.py:15
  137.8 0.0 copy-start.1
  137.8 0.4 convert_reduce_fusion
  138.1 0.0 copy-done
  138.1 1.1 fusion.7
  139.3 8.1 %all-to-all-start.2 = ((bf16[32,16,1,512]{3,1,2,0:T(8,128)(2,1)}), bf16[32,16,1,512]{3,1,2,0:T(8,128)(2,1)S(1)}, u32[]{:S(2)}, u32[]{:S(2)}) async-start(bf16[32,16,1,512]{3,1,2,0:T(8,128)(2,1)} %bitcast.16), calls=%async_computation.2 | async-start | bytes 1048576 | tf_op jit(solution)/shard_map/all_to_all | solution.py:15
  147.4 0.7 fusion.9
  148.1 17.6 %all-to-all-done.2 = bf16[32,16,1,512]{3,1,2,0:T(8,128)(2,1)S(1)} async-done(((bf16[32,16,1,512]{3,1,2,0:T(8,128)(2,1)}), bf16[32,16,1,512]{3,1,2,0:T(8,128)(2,1)S(1)}, u32[]{:S(2)}, u32[]{:S(2)}) %all-to-all-start.2) | async-done | bytes 524320 | tf_op jit(solution)/shard_map/all_to_all | solution.py:15
  165.7 0.1 convert_reduce_fusion.1
  165.8 0.0 copy-done.1
  165.8 0.6 bitcast_subtract_fusion
Async XLA Ops:
  7.2 90.5 %all-gather.3.cloned.1.call-start = ((), (), s32[]{:S(2)}) async-start(), calls=%async_computation.3 | async-start | bytes 8650752 | tf_op jit(solution)/shard_map/all_gather | solution.py:32
  104.7 33.4 %copy-start = (bf16[1,16,16,512]{3,2,1,0:T(8,128)(2,1)S(1)}, bf16[1,16,16,512]{3,2,1,0:T(8,128)(2,1)}, u32[]{:S(2)}) copy-start(bf16[1,16,16,512]{3,2,1,0:T(8,128)(2,1)} %param.5) | copy-start | bytes 786436
  137.8 28.1 %copy-start.1 = (f32[1,16,512]{2,1,0:T(8,128)S(1)}, f32[1,16,512]{2,1,0:T(8,128)}, u32[]{:S(2)}) copy-start(f32[1,16,512]{2,1,0:T(8,128)} %param.6) | copy-start | bytes 98308
  139.3 26.5 %all-to-all-start.2 = ((bf16[32,16,1,512]{3,1,2,0:T(8,128)(2,1)}), bf16[32,16,1,512]{3,1,2,0:T(8,128)(2,1)S(1)}, u32[]{:S(2)}, u32[]{:S(2)}) async-start(bf16[32,16,1,512]{3,1,2,0:T(8,128)(2,1)} %bitcast.16), calls=%async_computation.2 | async-start | bytes 1048576 | tf_op jit(solution)/shard_map/all_to_all | solution.py:15
Sparse Core Ops, SparseCore 0:
  19.9 77.6 all-gather.2
where the time goes:
time: 174 us; the launch traced here: 173 us
  waiting for transfers between devices  87.3 us (50%)
  blocking collectives  45.7 us (26%)
  between operations  14.1 us (8%)
  matrix products  8.13 us (5%)
  starting transfers between devices  8.12 us (5%)
  local copies, waits for them, and re-layouts  6.66 us (4%)
  other arithmetic  3.35 us (2%)
    all_gather x1, waiting for transfers between devices, on_device(): readers = lax.all_gather(received, 'blk', axis=2, tiled=True)  69.7 us
    all_to_all x1, blocking collectives, sum_at_owner(): tiles = lax.all_to_all(split_up(shard, dim, count), axis, 0, 0, tiled=True)  33.1 us
    all_to_all x1, waiting for transfers between devices, sum_at_owner(): tiles = lax.all_to_all(split_up(shard, dim, count), axis, 0, 0, tiled=True)  17.6 us
    all_to_all x1, blocking collectives, on_device(): lax.all_to_all(grouped, 'grp', split_axis=1, concat_axis=0, tiled=True)  12.6 us
    all_to_all x1, starting transfers between devices, sum_at_owner(): tiles = lax.all_to_all(split_up(shard, dim, count), axis, 0, 0, tiled=True)  8.09 us
    dot_general x1, matrix products, on_device(): jnp.einsum('crjxy,cjyz->crxz', selected, readers, preferred_element_type=...  6.99 us
    gather x1, local copies, waits for them, and re-layouts, on_device(): selected = inv_tiles[structure[:, :, None], local_cols[:, None, :]]  6.51 us
  transfers between devices with their start and end apart: 2, of which 2 were waited for; matrix products, arithmetic and copies ran while one was open for 5% of the time, Pallas kernels for 0%

commit v1 on v0

--- a/solution.py
+++ b/solution.py
@@ -29,7 +29,9 @@
     grouped = factor.reshape(own_count, grp_count, per_group, slab_rows, width)
     received = lax.all_to_all(grouped, "grp", split_axis=1, concat_axis=0, tiled=True)
     received = received.reshape(node_total, per_group, slab_rows, width)
-    readers = lax.all_gather(received, "blk", axis=2, tiled=True)
+    readers = jnp.concatenate(
+        lax.all_to_all(jnp.stack([received] * lax.axis_size("blk")), "blk", 0, 0), axis=2
+    )
     col_base = grp_index * col_local
     local_cols = lax.dynamic_slice_in_dim(structure, grp_index * per_group, per_group, 1) - col_base
     selected = inv_tiles[structure[:, :, None], local_cols[:, None, :]]

time: 174 us -> 289 us (1.66)
  waiting for transfers between devices: 87.3 us -> 195 us
  starting transfers between devices: 8.12 us -> 23 us
  between operations: 14.1 us -> 0.71 us
  local copies, waits for them, and re-layouts: 6.66 us -> 19.2 us
  blocking collectives: 45.7 us -> 41.7 us
    all_to_all x0 -> x1, waiting for transfers between devices: none -> 178 us  [on_device(): lax.all_to_all(jnp.stack([received] * lax.axis_size('blk')), 'blk', 0, 0)]
    all_gather x1 -> x0, waiting for transfers between devices: 69.7 us -> none  [on_device(): readers = lax.all_gather(received, 'blk', axis=2, tiled=True)]
    all_to_all x0 -> x1, starting transfers between devices: none -> 12.4 us  [on_device(): lax.all_to_all(jnp.stack([received] * lax.axis_size('blk')), 'blk', 0, 0)]
    reshape x0 -> x1, local copies, waits for them, and re-layouts: none -> 8.22 us  [on_device(): jnp.concatenate(lax.all_to_all(jnp.stack([received] * lax.axis_size('blk'...]
    another operation x0 -> x1, local copies, waits for them, and re-layouts: none -> 4.3 us  [on_device(): jnp.stack([received] * lax.axis_size('blk'))]
    all_to_all x1, blocking collectives: 33.1 us -> 29.2 us  [sum_at_owner(): tiles = lax.all_to_all(split_up(shard, dim, count), axis, 0, 0, tiled=True)]
  transfers between devices with their start and end apart: 2 -> 2, of which waited for: 2 -> 2; matrix products, arithmetic and copies ran while one was open for 5% -> 3% of each run, Pallas kernels for 0% -> 0%
where the time goes in v1:
time: 289 us
  waiting for transfers between devices  195 us (67%)
  blocking collectives  41.7 us (14%)
  starting transfers between devices  23 us (8%)
  local copies, waits for them, and re-layouts  19.2 us (7%)
  matrix products  6.86 us (2%)
    all_to_all x1, waiting for transfers between devices, on_device(): lax.all_to_all(jnp.stack([received] * lax.axis_size('blk')), 'blk', 0, 0)  178 us
    all_to_all x1, blocking collectives, sum_at_owner(): tiles = lax.all_to_all(split_up(shard, dim, count), axis, 0, 0, tiled=True)  29.2 us
    all_to_all x1, waiting for transfers between devices, sum_at_owner(): tiles = lax.all_to_all(split_up(shard, dim, count), axis, 0, 0, tiled=True)  17.6 us
    all_to_all x1, blocking collectives, on_device(): lax.all_to_all(grouped, 'grp', split_axis=1, concat_axis=0, tiled=True)  12.5 us
    all_to_all x1, starting transfers between devices, on_device(): lax.all_to_all(jnp.stack([received] * lax.axis_size('blk')), 'blk', 0, 0)  12.4 us
    all_to_all x1, starting transfers between devices, sum_at_owner(): tiles = lax.all_to_all(split_up(shard, dim, count), axis, 0, 0, tiled=True)  10.5 us
    reshape x1, local copies, waits for them, and re-layouts, on_device(): jnp.concatenate(lax.all_to_all(jnp.stack([received] * lax.axis_size('blk'...  8.22 us
    gather x1, local copies, waits for them, and re-layouts, on_device(): selected = inv_tiles[structure[:, :, None], local_cols[:, None, :]]  6.48 us
  transfers between devices with their start and end apart: 2, of which 2 were waited for; matrix products, arithmetic and copies ran while one was open for 3% of the time, Pallas kernels for 0%

profile of v1, /device:TPU:1, one launch (start us, length us, event | category | flops | bytes accessed | tf_op | source)
XLA Modules:
  0.0 288.8 jit_solution(210310976270969708)
XLA Ops:
  0.6 12.5 %all_to_all.24 = bf16[1,8,2,16,512]{4,3,2,0,1:T(8,128)(2,1)S(1)} all-to-all(bf16[1,8,2,16,512]{4,3,2,0,1:T(8,128)(2,1)} %bitcast.44), channel_id=1, replica_groups=mesh['blk'=32,'grp'=8] {'grp'}, dimensions={1} | all-to-all | bytes 524288 | tf_op jit(solution)/shard_map/all_to_all | solution.py:30
  13.1 4.3 %stack.3 = bf16[32,8,2,16,512]{4,3,2,1,0:T(8,128)(2,1)} broadcast(bf16[8,2,16,512]{3,2,1,0:T(8,128)(2,1)S(1)} %bitcast.45), dimensions={1,2,3,4} | broadcast | bytes 8650752 | tf_op jit(solution)/shard_map/stack | solution.py:33
  17.4 0.0 copy-start.3
  17.4 12.4 %all-to-all-start.1 = ((bf16[32,8,2,16,512]{4,3,2,1,0:T(8,128)(2,1)}), bf16[32,8,2,16,512]{4,3,2,1,0:T(8,128)(2,1)}, u32[]{:S(2)}, u32[]{:S(2)}) async-start(bf16[32,8,2,16,512]{4,3,2,1,0:T(8,128)(2,1)} %stack.3), calls=%async_computation.1 | async-start | bytes 16777216 | tf_op jit(solution)/shard_map/all_to_all | solution.py:33
  29.9 0.0 copy-done.3
  29.9 0.1 fusion.7
  30.0 0.1 broadcast_or_fusion
  30.1 0.1 reshape.69
  30.2 6.5 %gather_fusion = bf16[256,16,512]{2,1,0:T(8,128)(2,1)} fusion(bf16[64,8,16,512]{3,2,1,0:T(8,128)(2,1)} %param.4, s32[256]{0:T(256)S(1)} %reshape.69), kind=kCustom, calls=%fused_computation | custom fusion | bytes 8390656 | tf_op jit(solution)/shard_map/gather | solution.py:37
  36.7 177.7 %all-to-all-done.1 = bf16[32,8,2,16,512]{4,3,2,1,0:T(8,128)(2,1)} async-done(((bf16[32,8,2,16,512]{4,3,2,1,0:T(8,128)(2,1)}), bf16[32,8,2,16,512]{4,3,2,1,0:T(8,128)(2,1)}, u32[]{:S(2)}, u32[]{:S(2)}) %all-to-all-start.1) | async-done | bytes 8388640 | tf_op jit(solution)/shard_map/all_to_all | solution.py:33
  214.4 0.0 copy-start
  214.4 8.2 %copy.6 = bf16[8,2,32,16,512]{4,3,2,1,0:T(8,128)(2,1)} copy(bf16[8,2,32,16,512]{4,3,1,0,2:T(8,128)(2,1)} %bitcast.3) | data formatting | bytes 16777216 | tf_op jit(solution)/shard_map/reshape | solution.py:32
  222.6 0.0 copy-done
  222.6 5.7 %fusion = bf16[8,1,16,16,512]{4,3,2,1,0:T(8,128)(2,1)S(1)} fusion(bf16[8,16,2,16,512]{4,3,2,1,0:T(8,128)(2,1)S(1)} %bitcast.43, bf16[8,2,512,512,1]{3,2,1,4,0:T(8,128)(2,1)} %bitcast.42), kind=kOutput, calls=%fused_computation.3 | convolution fusion | flops 2148532224 | bytes 14680064 | tf_op jit(solution)/shard_map/crjxy,cjyz->crxz/dot_general | solution.py:39
  228.4 0.0 copy-start.1
  228.4 29.2 %all_to_all.25 = bf16[8,1,16,16,512]{4,3,2,1,0:T(8,128)(2,1)S(1)} all-to-all(bf16[8,1,16,16,512]{4,3,2,1,0:T(8,128)(2,1)S(1)} %fusion), channel_id=1, replica_groups=mesh['blk'=32,'grp'=8] {'grp'}, dimensions={0} | all-to-all | bytes 4194304 | tf_op jit(solution)/shard_map/all_to_all | solution.py:15
  257.6 0.0 copy-start.2
  257.6 0.4 convert_reduce_fusion
  258.0 0.0 copy-done.1
  258.0 1.2 fusion.1
  259.1 10.5 %all-to-all-start.3 = ((bf16[32,16,1,512]{3,1,2,0:T(8,128)(2,1)}), bf16[32,16,1,512]{3,1,2,0:T(8,128)(2,1)S(1)}, u32[]{:S(2)}, u32[]{:S(2)}) async-start(bf16[32,16,1,512]{3,1,2,0:T(8,128)(2,1)} %bitcast.17), calls=%async_computation.3 | async-start | bytes 1048576 | tf_op jit(solution)/shard_map/all_to_all | solution.py:15
  269.7 0.7 fusion.3
  270.4 17.6 %all-to-all-done.3 = bf16[32,16,1,512]{3,1,2,0:T(8,128)(2,1)S(1)} async-done(((bf16[32,16,1,512]{3,1,2,0:T(8,128)(2,1)}), bf16[32,16,1,512]{3,1,2,0:T(8,128)(2,1)S(1)}, u32[]{:S(2)}, u32[]{:S(2)}) %all-to-all-start.3) | async-done | bytes 524320 | tf_op jit(solution)/shard_map/all_to_all | solution.py:15
  288.0 0.1 convert_reduce_fusion.1
  288.1 0.0 copy-done.2
  288.1 0.6 bitcast_subtract_fusion
  (1 shorter events, 0.0 us)
Async XLA Ops:
  17.4 12.5 %copy-start.3 = (s32[8,16]{1,0:T(8,128)S(1)}, s32[8,16]{1,0:T(8,128)}, u32[]{:S(2)}) copy-start(s32[8,16]{1,0:T(8,128)} %param.7) | copy-start | bytes 1540
  17.4 197.0 %all-to-all-start.1 = ((bf16[32,8,2,16,512]{4,3,2,1,0:T(8,128)(2,1)}), bf16[32,8,2,16,512]{4,3,2,1,0:T(8,128)(2,1)}, u32[]{:S(2)}, u32[]{:S(2)}) async-start(bf16[32,8,2,16,512]{4,3,2,1,0:T(8,128)(2,1)} %stack.3), calls=%async_computation.1 | async-start | bytes 16777216 | tf_op jit(solution)/shard_map/all_to_all | solution.py:33
  214.4 8.2 %copy-start = (bf16[256,16,512]{2,1,0:T(8,128)(2,1)S(1)}, bf16[256,16,512]{2,1,0:T(8,128)(2,1)}, u32[]{:S(2)}) copy-start(bf16[256,16,512]{2,1,0:T(8,128)(2,1)} %gather_fusion) | copy-start | bytes 12582916
  228.4 29.6 %copy-start.1 = (bf16[1,16,16,512]{3,2,1,0:T(8,128)(2,1)S(1)}, bf16[1,16,16,512]{3,2,1,0:T(8,128)(2,1)}, u32[]{:S(2)}) copy-start(bf16[1,16,16,512]{3,2,1,0:T(8,128)(2,1)} %param.5) | copy-start | bytes 786436
  257.6 30.5 %copy-start.2 = (f32[1,16,512]{2,1,0:T(8,128)S(1)}, f32[1,16,512]{2,1,0:T(8,128)}, u32[]{:S(2)}) copy-start(f32[1,16,512]{2,1,0:T(8,128)} %param.6) | copy-start | bytes 98308
  259.1 28.9 %all-to-all-start.3 = ((bf16[32,16,1,512]{3,1,2,0:T(8,128)(2,1)}), bf16[32,16,1,512]{3,1,2,0:T(8,128)(2,1)S(1)}, u32[]{:S(2)}, u32[]{:S(2)}) async-start(bf16[32,16,1,512]{3,1,2,0:T(8,128)(2,1)} %bitcast.17), calls=%async_computation.3 | async-start | bytes 1048576 | tf_op jit(solution)/shard_map/all_to_all | solution.py:15
